TPU v7x, 32 devices: a whole 2x2x4 slice. The times are simulated.
32 devices in a mesh: sample: 4 (over y, x), seq: 4 (over z), head: 2 (over core).
Axes of the slice: x: 2, y: 2, z: 4, core: 2. Of those that a mesh axis runs over, the one named last changes fastest.
Arguments:
- values: bfloat16 [4, 2048, 4096], P('sample', 'seq', 'head'), may hold values from -6 to 6
- gate_values: bfloat16 [4, 2048, 4096], P('sample', 'seq', 'head'), may hold values from -6 to 6
- state_in: bfloat16 [4, 2048, 128], P('sample', 'seq'), may hold values from -0.5 to 0.5
- state_out: bfloat16 [4, 2048, 128], P('sample', 'seq'), may hold values from -0.5 to 0.5
- step_size: float32 [4, 2048, 64], P('sample', 'seq', 'head'), may hold values from 0.25 to 1
- log_decay: float32 [4, 2048, 64], P('sample', 'seq', 'head'), may hold values from -1 to 0, as said below
- skip_gain: float32 [64], P('head'), may hold values from 0.5 to 1.5
- norm_gain: float32 [4096], P('head'), may hold values from 0.25 to 1.75
- out_weight: bfloat16 [4096, 4096], P('head', 'seq'), may hold values from -0.09375 to 0.09375
- prompt_state: float32 [64, 64, 128], P('head', None, 'sample'), may hold values from -16 to 16
Outputs:
- projected: bfloat16 [4, 2048, 4096], P('sample', 'seq', 'head')
Inputs may be any that keep to these rules, and one draw needn't show every extreme that they name: `log_decay`: every entry is negative.
All inputs are finite; a program needn't handle non-finite values.
Results may differ from a plain program's by a relative error of at most 0.019.
Values may be sent and summed in bfloat16 or wider, within the bound.
No kernel may reach another device: no remote copies, remote signals or barrier semaphores. Data moves between devices by JAX's collectives and lax.ppermute only.
A program may use at most 128 MiB of HBM per device.

v0:
```python
from functools import partial
import jax
import jax.numpy as jnp
from jax import lax
from jax.sharding import PartitionSpec as P

P_SIZE = 64
L = 256
GROUP_HEADS = 8
EPSILON = 1e-05


def carried_in(array, axis, join, neutral):
    place = lax.axis_index(axis)
    gathered = jax.tree.map(
        lambda a, kind: lax.all_gather(a.astype(kind), axis), array, (jnp.bfloat16, jnp.bfloat16)
    )
    state = jax.tree.map(lambda a, e: jnp.zeros_like(a) + jnp.asarray(e, a.dtype), array, neutral)

    def one(step, state):
        return join(
            state,
            jax.tree.map(
                lambda a, own: lax.dynamic_index_in_dim(a, step, 0, False).astype(own.dtype),
                gathered,
                array,
            ),
        )

    return lax.fori_loop(0, place, one, state)


def block_terms(values_blk, in_blk, out_blk, step_blk, decay_blk, skip_gain):
    heads = decay_blk.shape[1]
    running = jnp.cumsum(decay_blk, axis=0)
    per_head = values_blk.reshape(values_blk.shape[0], heads, -1)
    scaled = (per_head.astype(jnp.float32) * step_blk[:, :, None]).astype(jnp.bfloat16)
    scores = jnp.dot(out_blk, in_blk.T, preferred_element_type=jnp.float32)
    token_offset = jnp.arange(values_blk.shape[0])
    causal = token_offset[:, None] >= token_offset[None, :]
    by_head = running.T
    spread = by_head[:, :, None] - by_head[:, None, :]
    pair_decay = jnp.exp(jnp.where(causal[None], spread, -1e30))
    mixing = (scores[None] * pair_decay).astype(jnp.bfloat16)
    inner = jnp.einsum("hts,shp->thp", mixing, scaled, preferred_element_type=jnp.float32)
    tail = jnp.exp(running[-1][None, :] - running)
    weighted = (scaled.astype(jnp.float32) * tail[:, :, None]).astype(jnp.bfloat16)
    block_state = jnp.einsum("shp,sn->hpn", weighted, in_blk, preferred_element_type=jnp.float32)
    local_out = inner + skip_gain[None, :, None] * per_head.astype(jnp.float32)
    return (local_out, running, block_state)


def local_sweep(values_s, in_s, out_s, step_s, decay_s, skip_gain):
    count = values_s.shape[0] // L
    heads = decay_s.shape[1]
    width = values_s.shape[1] // heads
    states = in_s.shape[1]
    blocks = (
        values_s.reshape(count, L, -1),
        in_s.reshape(count, L, -1),
        out_s.reshape(count, L, -1),
        step_s.reshape(count, L, heads),
        decay_s.reshape(count, L, heads),
    )

    def advance(carry, block):
        state, total = carry
        values_blk, in_blk, out_blk, step_blk, decay_blk = block
        local_out, running, block_state = block_terms(
            values_blk, in_blk, out_blk, step_blk, decay_blk, skip_gain
        )
        new_state = jnp.exp(running[-1])[:, None, None] * state + block_state
        return ((new_state, total + running[-1]), (local_out, running, state, total))

    initial = (jnp.zeros((heads, width, states), jnp.float32), jnp.zeros((heads,), jnp.float32))
    return lax.scan(advance, initial, blocks)


def link(earlier, later):
    decay_early, state_early = earlier
    decay_late, state_late = later
    return (decay_early * decay_late, decay_late[:, :, None, None] * state_early + state_late)


def group_norm(gated, norm_gain):
    width = GROUP_HEADS * P_SIZE
    grouped = gated.reshape(gated.shape[0], -1, width)
    mean_square = jnp.mean(grouped * grouped, axis=-1, keepdims=True)
    rescaled = grouped * lax.rsqrt(mean_square + EPSILON)
    return (rescaled.reshape(gated.shape) * norm_gain).astype(jnp.bfloat16)


def shards(
    values,
    gate_values,
    state_in,
    state_out,
    step_size,
    log_decay,
    skip_gain,
    norm_gain,
    out_weight,
    prompt_state,
):
    prompt = lax.all_gather(prompt_state.astype(jnp.bfloat16), "sample", axis=2, tiled=True).astype(
        prompt_state.dtype
    )
    sweep_sample = partial(local_sweep, skip_gain=skip_gain)
    (last_state, last_total), (local_out, running, before, totals) = jax.vmap(sweep_sample)(
        values, state_in, state_out, step_size, log_decay
    )
    identity = (jnp.ones_like(last_total), jnp.zeros_like(last_state))
    lead_decay, lead_state = carried_in((jnp.exp(last_total), last_state), "seq", link, identity)
    entry = lead_state + lead_decay[:, :, None, None] * prompt[None]
    start = before + jnp.exp(totals)[:, :, :, None, None] * entry[:, None]
    start_low = start.astype(jnp.bfloat16)
    samples, tokens = (values.shape[0], values.shape[1])
    count = tokens // L
    out_blocks = state_out.reshape(samples, count, L, -1)
    carried = jnp.exp(running)[..., None] * jnp.einsum(
        "sktn,skhpn->skthp", out_blocks, start_low, preferred_element_type=jnp.float32
    )
    outputs = (local_out + carried).reshape(samples * tokens, -1)
    gated = outputs * jax.nn.silu(gate_values.reshape(samples * tokens, -1).astype(jnp.float32))
    normed = group_norm(gated, norm_gain)
    terms = jnp.dot(
        normed,
        lax.all_gather(out_weight, "seq", axis=1, tiled=True),
        preferred_element_type=jnp.float32,
    )
    mine = lax.psum_scatter(terms.astype(jnp.bfloat16), "head", scatter_dimension=1, tiled=True)
    return mine.reshape(samples, tokens, -1)


def solution(mesh):
    in_specs = (
        P("sample", "seq", "head"),
        P("sample", "seq", "head"),
        P("sample", "seq", None),
        P("sample", "seq", None),
        P("sample", "seq", "head"),
        P("sample", "seq", "head"),
        P("head"),
        P("head"),
        P("head", "seq"),
        P("head", None, "sample"),
    )
    out_specs = P("sample", "seq", "head")
    return jax.shard_map(shards, mesh=mesh, in_specs=in_specs, out_specs=out_specs, check_vma=False)
```

profile of v0, /device:TPU:0, one launch (start us, length us, event | category | flops | bytes accessed | tf_op | source)
XLA Modules:
  0.0 398.6 jit_solution(10033825159931947701)
XLA Ops:
  6.5 0.9 reshape.287
  7.4 0.9 reshape.289
  8.3 22.4 %while.34 = (s32[]{:T(128)}, f32[1,32,64,128]{3,2,1,0:T(8,128)S(1)}, f32[1,32]{1,0:T(1,128)S(1)}, f32[2,1,256,32,64]{2,4,3,1,0:T(8,128)}, f32[2,1,256,32]{2,0,3,...) while((s32[]{:T(128)}, ...), condition=%wide.region_3.4_spmd.clone, body=%wide.region_0.3_spmd.clone.sunk | while | flops 435765440 | bytes 33923384 | solution.py:76
  8.4 0.1 constant_dynamic-slice_fusion.6
  8.5 0.6 reduce-window.14
  9.1 0.2 slice_reduce_fusion.4
  9.3 0.1 copy.88
  9.4 0.1 broadcast.141
  9.6 1.3 constant_dynamic-slice_fusion.7
  10.9 0.5 copy.91
  11.4 0.2 convert_element_type.202
  11.6 0.2 fusion.48
  11.8 3.7 fusion.49
  15.6 0.5 slice_reduce_fusion.5
  16.1 0.1 subtract_exponential_fusion.2
  16.3 0.2 mul.298
  16.4 0.2 mul.299
  16.6 0.5 multiply_convert_fusion.13
  17.1 1.0 bitcast_dynamic-update-slice_fusion.2
  18.2 0.5 fusion.47
  18.7 0.2 dynamic_update_slice.30
  18.9 0.6 copy-done.9
  19.5 0.1 constant_dynamic-slice_fusion.6
  19.6 0.6 reduce-window.14
  20.2 0.2 slice_reduce_fusion.4
  20.4 0.1 copy.88
  20.5 0.1 broadcast.141
  20.7 1.3 constant_dynamic-slice_fusion.7
  22.0 0.5 copy.91
  22.5 0.2 convert_element_type.202
  22.7 0.2 fusion.48
  23.0 3.8 fusion.49
  26.8 0.5 slice_reduce_fusion.5
  27.3 0.1 subtract_exponential_fusion.2
  27.4 0.2 mul.298
  27.6 0.2 mul.299
  27.8 0.5 multiply_convert_fusion.13
  28.3 1.0 bitcast_dynamic-update-slice_fusion.2
  29.4 0.5 fusion.47
  29.9 0.2 dynamic_update_slice.30
  30.0 0.6 copy-done.9
  30.7 0.9 convert_element_type.137
  31.6 0.0 all-gather.6.cloned.1.call-start
  31.6 0.7 all-gather.6.cloned.1.call-update
  32.3 0.0 reduce-scatter.2.cloned.1.call-start
  32.4 0.3 copy.72
  32.8 2.9 copy.55
  35.7 4.0 reshape.301
  39.7 12.9 %all-gather.2 = bf16[4,1,32]{2,1,0:T(2,128)(2,1)S(1)} all-gather(bf16[1,1,32]{2,1,0:T(2,128)(2,1)S(1)} %convert_bitcast_fusion.1), channel_id=2, replica_groups=mesh['sample'=4,'seq'=4,'head'=2] {'seq'}, dimensions={0}, use_global_device_ids=true | all-gather | bytes 320 | tf_op jit(solution)/shard_map/all_gather | solution.py:16
  52.6 13.7 %all_gather.22 = bf16[32,64,128]{1,0,2:T(8,128)(2,1)} all-gather(bf16[32,64,32]{1,0,2:T(8,128)(2,1)S(1)} %copy.72), channel_id=1, replica_groups=mesh['sample'=4,'seq'=4,'head'=2] {'sample'}, dimensions={2}, use_global_device_ids=true | all-gather | bytes 655360 | tf_op jit(solution)/shard_map/all_gather | solution.py:105
  66.3 13.9 %all-gather.8.cloned.1.call-done = bf16[4,32,64,128]{3,2,1,0:T(8,128)(2,1)} async-done(((bf16[1,32,64,128]{3,2,1,0:T(8,128)(2,1)}), bf16[4,32,64,128]{3,2,1,0:T(8,128)(2,1)}) %all-gather.8.cloned.1.call-update) | async-done | bytes 2097168 | tf_op jit(solution)/shard_map/all_gather | solution.py:16
  80.1 0.1 broadcast.97
  80.3 2.8 copy.52
  83.1 3.6 fusion.27
  86.8 3.0 copy.53
  89.8 6.7 %multiply_reduce_fusion = (f32[2,256,32]{1,2,0:T(8,128)S(1)}, f32[2,256,32,64]{1,3,2,0:T(8,128)S(1)}) fusion(f32[2,256,32,64]{1,0,3,2:T(2,128)} %reshape.301, bf16[2,256,128,1]{2,1,3,0:T(8,128)(2,1)S(1)} %bitcast.226, f32[2,1,32,64,128]{4,3,2,1,0:T(8,128)} %get-tuple-element.113, f32[32,64,128]{2,1,0:T(8,128)S(1)} %copy.53, f32[2,32]{1,0:T(2,128)S(1)} %bitcast.229, ...), kind=kOutput, calls=%fused_computation.59 | convolution fusion | flops 279429120 | bytes 15991040 | tf_op jit(solution)/shard_map/sktn,skhpn->skthp/dot_general | solution.py:120
  96.6 3.4 copy.54
  99.9 2.4 copy.65
  102.3 0.1 copy.58
  102.4 0.1 reduce_sum.14
  102.5 4.0 %fusion.21 = bf16[512,2048]{0,1:T(8,128)(2,1)} fusion(f32[512,2048]{0,1:T(8,128)} %bitcast.212, f32[2048]{0:T(1024)S(1)} %copy-done.11, f32[512,4]{0,1:T(4,128)S(1)} %add_rsqrt_fusion, bf16[1,512,2048]{1,2,0:T(8,128)(2,1)S(1)} %copy.55), kind=kLoop, calls=%fused_computation.50 | loop fusion | flops 9437184 | bytes 8404992 | tf_op jit(solution)/shard_map/convert_element_type | solution.py:90
  106.5 260.8 %all-gather.6.cloned.1.call-done = bf16[2048,4096]{1,0:T(8,128)(2,1)} async-done(((bf16[2048,1024]{1,0:T(8,128)(2,1)}), bf16[2048,4096]{1,0:T(8,128)(2,1)}) %all-gather.6.cloned.1.call-update) | async-done | bytes 16777232 | tf_op jit(solution)/shard_map/all_gather | solution.py:128
  367.3 14.6 %convolution_convert_fusion = bf16[512,4096]{1,0:T(8,128)(2,1)} fusion(bf16[512,2048]{0,1:T(8,128)(2,1)} %fusion.21, bf16[2048,4096]{1,0:T(8,128)(2,1)} %all-gather.6.cloned.1.call-done), kind=kOutput, calls=%fused_computation.47 | convolution fusion | flops 8592031744 | bytes 23068672 | tf_op jit(solution)/shard_map/dot_general | solution.py:126
  381.9 10.2 %reduce-scatter.2.cloned.1.call-done = bf16[512,2048]{1,0:T(8,128)(2,1)} async-done(((bf16[512,4096]{1,0:T(8,128)(2,1)}), bf16[512,2048]{1,0:T(8,128)(2,1)}) %reduce-scatter.2.cloned.1.call-update) | async-done | bytes 2097168 | tf_op jit(solution)/shard_map/reduce_scatter | solution.py:131
  (85 shorter events, 0.7 us)
Async XLA Ops:
  6.5 73.6 %all-gather.8.cloned.1.call-start = ((), (), s32[]{:S(2)}) async-start(), calls=%async_computation.3 | async-start | bytes 2621440 | tf_op jit(solution)/shard_map/all_gather | solution.py:16
  8.3 1.2 copy-start.3
  8.3 1.2 copy-start.5
  8.3 3.2 copy-start
  8.4 3.2 copy-start.1
  8.4 3.4 copy-start.12
  17.1 1.6 copy-start.8
  17.1 2.4 copy-start.4
  17.1 2.4 copy-start.6
  18.8 0.6 copy-start.9
  19.5 1.2 copy-start.3
  19.5 1.2 copy-start.5
  19.5 3.2 copy-start
  19.5 3.2 copy-start.1
  19.5 3.4 copy-start.12
  28.3 1.6 copy-start.8
  28.3 2.4 copy-start.4
  28.3 2.4 copy-start.6
  30.0 0.6 copy-start.9
  30.7 1.7 copy-start.7
  30.7 2.0 copy-start.10
  31.6 335.7 %all-gather.6.cloned.1.call-start = ((), (), s32[]{:S(2)}) async-start(), calls=%async_computation.1 | async-start | bytes 20971520 | tf_op jit(solution)/shard_map/all_gather | solution.py:128
  32.3 359.8 %reduce-scatter.2.cloned.1.call-start = ((), (), s32[]{:S(2)}) async-start(), calls=%async_computation.2 | async-start | bytes 6291456 | tf_op jit(solution)/shard_map/reduce_scatter | solution.py:131
  83.1 6.6 %copy-start.2 = (bf16[2,1,256,128]{3,2,1,0:T(8,128)(2,1)S(1)}, bf16[2,1,256,128]{3,2,1,0:T(8,128)(2,1)}, u32[]{:S(2)}) copy-start(bf16[2,1,256,128]{3,2,1,0:T(8,128)(2,1)} %get-tuple-element.478) | copy-start | bytes 393220
  99.9 2.6 copy-start.11
Sparse Core Ops, SparseCore 0:
  31.7 48.4 all-gather.7
  81.7 285.5 all-gather.5
  382.0 10.0 reduce-scatter.1
where the time goes:
time: 399 us
  waiting for transfers between devices  286 us (72%)
  matrix products  30.1 us (8%)
  local copies, waits for them, and re-layouts  28.7 us (7%)
  blocking collectives  26.6 us (7%)
  other arithmetic  13.7 us (3%)
  between operations  13.3 us (3%)
    all_gather x1, waiting for transfers between devices, shards(): lax.all_gather(out_weight, 'seq', axis=1, tiled=True)  261 us
    dot_general x1, matrix products, shards(): jnp.dot(normed, lax.all_gather(out_weight, 'seq', axis=1, tiled=True), pr...  14.6 us
    all_gather x1, waiting for transfers between devices, carried_in(): lax.all_gather(a.astype(kind), axis)  13.9 us
    all_gather x1, blocking collectives, shards(): lax.all_gather(prompt_state.astype(jnp.bfloat16), 'sample', axis=2, tiled...  13.7 us
    all_gather x1, blocking collectives, carried_in(): lax.all_gather(a.astype(kind), axis)  12.9 us
    reduce_scatter x1, waiting for transfers between devices, shards(): lax.psum_scatter(terms.astype(jnp.bfloat16), 'head', scatter_dimension=1,...  10.2 us
  transfers between devices with their start and end apart: 3, of which 3 were waited for; matrix products, arithmetic and copies ran while one was open for 8% of the time, Pallas kernels for 0%

commit v1 on v0

--- a/solution.py
+++ b/solution.py
@@ -3,6 +3,7 @@
 import jax.numpy as jnp
 from jax import lax
 from jax.sharding import PartitionSpec as P
+from jax.lax import all_gather
 
 P_SIZE = 64
 L = 256
@@ -123,11 +124,8 @@
     outputs = (local_out + carried).reshape(samples * tokens, -1)
     gated = outputs * jax.nn.silu(gate_values.reshape(samples * tokens, -1).astype(jnp.float32))
     normed = group_norm(gated, norm_gain)
-    terms = jnp.dot(
-        normed,
-        lax.all_gather(out_weight, "seq", axis=1, tiled=True),
-        preferred_element_type=jnp.float32,
-    )
+    find_shifts_all = lambda field_in: jnp.concatenate(all_gather(field_in, axis_name="seq"), 1)
+    terms = jnp.dot(normed, find_shifts_all(out_weight), preferred_element_type=jnp.float32)
     mine = lax.psum_scatter(terms.astype(jnp.bfloat16), "head", scatter_dimension=1, tiled=True)
     return mine.reshape(samples, tokens, -1)
 

time: 399 us -> 421 us (1.055)
  local copies, waits for them, and re-layouts: 28.7 us -> 57.3 us
  waiting for transfers between devices: 286 us -> 279 us
    reshape x2 -> x4, local copies, waits for them, and re-layouts: 0.01 us -> 28.3 us  [the longest x1 21.8 us: shards(): jnp.concatenate(all_gather(field_in, axis_name='seq'), 1)]
    unnamed x11, local copies, waits for them, and re-layouts: 5.58 us -> 0.54 us
    convert_element_type x1 -> x2, local copies, waits for them, and re-layouts: 3.99 us -> 8.86 us  [shards(): gate_values.reshape(samples * tokens, -1).astype(jnp.float32)]
    all_gather x1, waiting for transfers between devices: 261 us -> 256 us  [shards(): all_gather(field_in, axis_name='seq')]
  transfers between devices with their start and end apart: 3 -> 3, of which waited for: 3 -> 3; matrix products, arithmetic and copies ran while one was open for 8% -> 10% of each run, Pallas kernels for 0% -> 0%
where the time goes in v1:
time: 421 us; the launch traced here: 420 us
  waiting for transfers between devices  279 us (66%)
  local copies, waits for them, and re-layouts  57.3 us (14%)
  matrix products  29.7 us (7%)
  blocking collectives  26.4 us (6%)
  other arithmetic  13.3 us (3%)
  between operations  13.3 us (3%)
    all_gather x1, waiting for transfers between devices, shards(): all_gather(field_in, axis_name='seq')  256 us
    reshape x1, local copies, waits for them, and re-layouts, shards(): jnp.concatenate(all_gather(field_in, axis_name='seq'), 1)  21.8 us
    dot_general x1, matrix products, shards(): jnp.dot(normed, find_shifts_all(out_weight), preferred_element_type=jnp.f...  13.9 us
    all_gather x1, blocking collectives, shards(): lax.all_gather(prompt_state.astype(jnp.bfloat16), 'sample', axis=2, tiled...  13.3 us
    all_gather x1, blocking collectives, carried_in(): lax.all_gather(a.astype(kind), axis)  13.1 us
    all_gather x1, waiting for transfers between devices, carried_in(): lax.all_gather(a.astype(kind), axis)  11.9 us
    reduce_scatter x1, waiting for transfers between devices, shards(): lax.psum_scatter(terms.astype(jnp.bfloat16), 'head', scatter_dimension=1,...  10.2 us
    convert_element_type x2, local copies, waits for them, and re-layouts, shards(): gate_values.reshape(samples * tokens, -1).astype(jnp.float32)  8.86 us
  transfers between devices with their start and end apart: 3, of which 3 were waited for; matrix products, arithmetic and copies ran while one was open for 10% of the time, Pallas kernels for 0%

profile of v1, /device:TPU:0, one launch (start us, length us, event | category | flops | bytes accessed | tf_op | source)
XLA Modules:
  0.0 419.8 jit_solution(17606641393341831787)
XLA Ops:
  6.5 0.9 reshape.340
  7.4 0.9 reshape.342
  8.3 22.3 %while.34 = (s32[]{:T(128)}, f32[1,32,64,128]{3,2,1,0:T(8,128)S(1)}, f32[1,32]{1,0:T(1,128)S(1)}, f32[2,1,256,32,64]{2,4,3,1,0:T(8,128)}, f32[2,1,256,32]{2,0,3,...) while((s32[]{:T(128)}, ...), condition=%wide.region_3.4_spmd.clone, body=%wide.region_0.3_spmd.clone.sunk | while | flops 435765440 | bytes 33923384 | solution.py:77
  8.4 0.1 constant_dynamic-slice_fusion.6
  8.5 0.6 reduce-window.14
  9.1 0.2 slice_reduce_fusion.4
  9.3 0.1 copy.92
  9.4 0.1 broadcast.168
  9.6 1.3 constant_dynamic-slice_fusion.7
  10.9 0.5 copy.95
  11.4 0.2 convert_element_type.218
  11.6 0.2 fusion.42
  11.8 3.7 fusion.43
  15.6 0.5 slice_reduce_fusion.5
  16.1 0.1 subtract_exponential_fusion.2
  16.3 0.2 mul.314
  16.4 0.2 mul.315
  16.6 0.5 multiply_convert_fusion.14
  17.1 1.0 bitcast_dynamic-update-slice_fusion.2
  18.2 0.5 fusion.41
  18.7 0.2 dynamic_update_slice.30
  18.9 0.6 copy-done.10
  19.5 0.1 constant_dynamic-slice_fusion.6
  19.6 0.6 reduce-window.14
  20.2 0.2 slice_reduce_fusion.4
  20.4 0.1 copy.92
  20.5 0.1 broadcast.168
  20.7 1.3 constant_dynamic-slice_fusion.7
  22.0 0.5 copy.95
  22.5 0.2 convert_element_type.218
  22.7 0.2 fusion.42
  23.0 3.7 fusion.43
  26.8 0.5 slice_reduce_fusion.5
  27.3 0.1 subtract_exponential_fusion.2
  27.4 0.2 mul.314
  27.6 0.2 mul.315
  27.7 0.5 multiply_convert_fusion.14
  28.3 1.0 bitcast_dynamic-update-slice_fusion.2
  29.3 0.5 fusion.41
  29.8 0.2 dynamic_update_slice.30
  30.0 0.6 copy-done.10
  30.6 0.9 convert_element_type.153
  31.6 0.7 all-gather.9.cloned.1.call-update
  32.4 0.2 copy-done.8
  32.6 0.3 copy.76
  33.0 3.0 copy.58
  35.9 5.9 %reshape.356 = f32[2,256,32,64]{1,0,3,2:T(2,128)} reshape(f32[1,512,2048]{1,2,0:T(8,128)} %copy.58) | data formatting | bytes 8388608 | tf_op jit(solution)/shard_map/convert_element_type | solution.py:125
  41.9 13.1 %all-gather.3 = bf16[4,1,32]{2,1,0:T(2,128)(2,1)S(1)} all-gather(bf16[1,1,32]{2,1,0:T(2,128)(2,1)S(1)} %convert_bitcast_fusion.1), channel_id=2, replica_groups=mesh['sample'=4,'seq'=4,'head'=2] {'seq'}, dimensions={0}, use_global_device_ids=true | all-gather | bytes 320 | tf_op jit(solution)/shard_map/all_gather | solution.py:17
  55.0 13.3 %all_gather.25 = bf16[32,64,128]{1,0,2:T(8,128)(2,1)} all-gather(bf16[32,64,32]{1,0,2:T(8,128)(2,1)S(1)} %copy.76), channel_id=1, replica_groups=mesh['sample'=4,'seq'=4,'head'=2] {'sample'}, dimensions={2}, use_global_device_ids=true | all-gather | bytes 655360 | tf_op jit(solution)/shard_map/all_gather | solution.py:106
  68.3 11.9 %all-gather.7.cloned.1.call-done = bf16[4,32,64,128]{3,2,1,0:T(8,128)(2,1)} async-done(((bf16[1,32,64,128]{3,2,1,0:T(8,128)(2,1)}), bf16[4,32,64,128]{3,2,1,0:T(8,128)(2,1)}) %all-gather.7.cloned.1.call-update) | async-done | bytes 2097168 | tf_op jit(solution)/shard_map/all_gather | solution.py:17
  80.1 0.1 broadcast.124
  80.3 1.8 copy.55
  82.1 3.0 fusion.21
  85.1 2.7 copy.56
  87.8 7.0 %multiply_reduce_fusion = (f32[2,256,32]{1,2,0:T(8,128)S(1)}, f32[2,256,32,64]{1,3,2,0:T(8,128)S(1)}) fusion(f32[2,256,32,64]{1,0,3,2:T(2,128)} %reshape.356, bf16[2,256,128,1]{2,1,3,0:T(8,128)(2,1)S(1)} %bitcast.210, f32[2,1,32,64,128]{4,3,2,1,0:T(8,128)} %get-tuple-element.113, f32[32,64,128]{2,1,0:T(8,128)S(1)} %copy.56, f32[2,32]{1,0:T(2,128)S(1)} %bitcast.213, ...), kind=kOutput, calls=%fused_computation.51 | convolution fusion | flops 279429120 | bytes 15991040 | tf_op jit(solution)/shard_map/sktn,skhpn->skthp/dot_general | solution.py:121
  94.8 5.2 %copy.57 = f32[2,256,32,64]{1,0,3,2:T(2,128)} copy(f32[2,256,32,64]{1,3,2,0:T(8,128)S(1)} %get-tuple-element.267) | data formatting | bytes 8388608 | tf_op jit(solution)/shard_map/add | solution.py:124
  100.0 6.5 %reshape.346 = f32[512,4,512]{0,2,1:T(8,128)} reshape(f32[2,256,32,64]{1,0,3,2:T(2,128)} %copy.57) | data formatting | bytes 8388608 | tf_op jit(solution)/shard_map/reshape | solution.py:124
  106.5 0.1 copy.62
  106.6 0.1 reduce_sum.14
  106.7 4.3 %multiply_convert_fusion.8 = bf16[512,4,512]{0,2,1:T(8,128)(2,1)S(1)} fusion(f32[512,4,512]{0,2,1:T(8,128)} %reshape.346, f32[512,4,512]{0,2,1:T(8,128)} %bitcast.194, f32[4,512]{1,0:T(4,128)S(1)} %mul.210, f32[512,4]{0,1:T(4,128)S(1)} %add_rsqrt_fusion), kind=kLoop, calls=%fused_computation.50 | loop fusion | flops 8388608 | bytes 10502144 | tf_op jit(solution)/shard_map/convert_element_type | solution.py:91
  110.9 256.3 %all-gather.9.cloned.1.call-done = bf16[8192,1024]{1,0:T(8,128)(2,1)} async-done(((bf16[2048,1024]{1,0:T(8,128)(2,1)}), bf16[8192,1024]{1,0:T(8,128)(2,1)}) %all-gather.9.cloned.1.call-update) | async-done | bytes 16777232 | tf_op jit(solution)/shard_map/all_gather | solution.py:127
  367.3 21.8 %copy.63 = bf16[2048,4,1024]{0,2,1:T(8,128)(2,1)} copy(bf16[2048,4,1024]{2,0,1:T(8,128)(2,1)} %bitcast.195) | data formatting | bytes 33554432 | tf_op jit(solution)/shard_map/reshape | solution.py:127
  389.1 13.9 %convolution_convert_fusion = bf16[512,4096]{1,0:T(8,128)(2,1)} fusion(bf16[512,2048]{0,1:T(8,128)(2,1)S(1)} %bitcast.208, bf16[2048,4096]{0,1:T(8,128)(2,1)} %bitcast.196), kind=kOutput, calls=%fused_computation.47 | convolution fusion | flops 8592031744 | bytes 23068672 | tf_op jit(solution)/shard_map/dot_general | solution.py:128
  403.0 10.2 %reduce-scatter.2.cloned.1.call-done = bf16[512,2048]{1,0:T(8,128)(2,1)} async-done(((bf16[512,4096]{1,0:T(8,128)(2,1)}), bf16[512,2048]{1,0:T(8,128)(2,1)}) %reduce-scatter.2.cloned.1.call-update) | async-done | bytes 2097168 | tf_op jit(solution)/shard_map/reduce_scatter | solution.py:129
  (89 shorter events, 0.8 us)
Async XLA Ops:
  6.5 73.6 %all-gather.7.cloned.1.call-start = ((), (), s32[]{:S(2)}) async-start(), calls=%async_computation.2 | async-start | bytes 2621440 | tf_op jit(solution)/shard_map/all_gather | solution.py:17
  8.3 1.2 copy-start.4
  8.3 1.2 copy-start.6
  8.3 3.2 copy-start
  8.4 3.2 copy-start.2
  8.4 3.4 copy-start.13
  17.1 1.6 copy-start.9
  17.1 2.4 copy-start.5
  17.1 2.4 copy-start.7
  18.8 0.6 copy-start.10
  19.5 1.2 copy-start.4
  19.5 1.2 copy-start.6
  19.5 3.2 copy-start
  19.5 3.2 copy-start.2
  19.5 3.4 copy-start.13
  28.2 1.6 copy-start.9
  28.2 2.4 copy-start.5
  28.2 2.4 copy-start.7
  30.0 0.6 copy-start.10
  30.6 2.2 copy-start.11
  30.6 2.3 copy-start.1
  31.5 1.0 copy-start.8
  31.6 335.7 %all-gather.9.cloned.1.call-start = ((), (), s32[]{:S(2)}) async-start(), calls=%async_computation.3 | async-start | bytes 20971520 | tf_op jit(solution)/shard_map/all_gather | solution.py:127
  32.3 380.9 %reduce-scatter.2.cloned.1.call-start = ((), (), s32[]{:S(2)}) async-start(), calls=%async_computation.1 | async-start | bytes 6291456 | tf_op jit(solution)/shard_map/reduce_scatter | solution.py:129
  35.9 5.9 %copy-start.12 = (f32[2048]{0:T(1024)S(1)}, f32[2048]{0:T(1024)}, u32[]{:S(2)}) copy-start(f32[2048]{0:T(1024)} %param.21) | copy-start | bytes 24580
  82.1 5.7 %copy-start.3 = (bf16[2,1,256,128]{3,2,1,0:T(8,128)(2,1)S(1)}, bf16[2,1,256,128]{3,2,1,0:T(8,128)(2,1)}, u32[]{:S(2)}) copy-start(bf16[2,1,256,128]{3,2,1,0:T(8,128)(2,1)} %get-tuple-element.479) | copy-start | bytes 393220
Sparse Core Ops, SparseCore 0:
  31.7 48.4 all-gather.6
  81.7 285.5 all-gather.8
  403.1 10.0 reduce-scatter.1
